TPU v7x, 32 devices: a whole 2x2x4 slice. The times are simulated.
32 devices in a mesh: rep: 2 (over y), seq: 8 (over z, x), head: 2 (over core).
Axes of the slice: x: 2, y: 2, z: 4, core: 2. Of those that a mesh axis runs over, the one named last changes fastest.
Arguments:
- x_in: bfloat16 [1024, 1024], P(('rep', 'seq'), 'head'), parts along dimension 0, may hold values from -6 to 6
- b_in: bfloat16 [1024, 2048], P(('rep', 'seq'), 'head'), parts along dimension 0, may hold values from -6 to 6
- c_in: bfloat16 [1024, 2048], P(('rep', 'seq'), 'head'), parts along dimension 0, may hold values from -6 to 6
- z_in: bfloat16 [1024, 1024], P(('rep', 'seq'), 'head'), parts along dimension 0, may hold values from -6 to 6
- dt_raw: bfloat16 [1024, 16], P(('rep', 'seq'), 'head'), parts along dimension 0, may hold values from -3 to 6
- dt_bias: float32 [16], P('head'), may hold values from -4 to -3
- a_log: float32 [16], P('head')
- d_skip: float32 [16], P('head'), may hold values from 0.5 to 1.5
- conv_x: bfloat16 [4, 1024], P(None, 'head'), may hold values from -3 to 3
- conv_b: bfloat16 [4, 2048], P(None, 'head'), may hold values from -3 to 3
- conv_c: bfloat16 [4, 2048], P(None, 'head'), may hold values from -3 to 3
- norm_gain: float32 [1024], P('head'), may hold values from 0.5 to 1.5
Outputs:
- mixed: bfloat16 [1024, 1024], P(('rep', 'seq'), 'head'), parts along dimension 0
There are 2 independent parts, one for each index of `rep`. A program takes and returns all parts, laid end to end along the dimension named above; an argument that names none is the same for every part. Nothing has to cross between parts.
All inputs are finite; a program needn't handle non-finite values.
Results may differ from a plain program's by a relative error of at most 0.0051.
Values may be sent and summed in bfloat16 or wider, within the bound.
No kernel may reach another device: no remote copies, remote signals or barrier semaphores. Data moves between devices by JAX's collectives and lax.ppermute only.
A program may use at most 64 MiB of HBM per device.

v0:
```python
import functools

import jax
import jax.numpy as jnp
from jax import lax
from jax.experimental import pallas as pl
from jax.experimental.pallas import tpu as pltpu
from jax.sharding import PartitionSpec as P


HEAD_DIM = 64
STATE = 256
BLOCK = 256
LANES = 128
HALO = 8
EDGE = 16
ORDER = (3, 2, 1)
RETURN = (3, 2, 1)
SPLIT = (1,)
F32 = jnp.float32
BF16 = jnp.bfloat16
VMEM = pl.BlockSpec(memory_space=pltpu.VMEM)
HBM = pl.BlockSpec(memory_space=pltpu.HBM)
NT = (((1,), (1,)), ((), ()))
TN = (((0,), (0,)), ((), ()))
NN = (((1,), (0,)), ((), ()))


def dot(a, b, dims):
    return lax.dot_general(a, b, dims, preferred_element_type=F32)


class Sizes:
    def __init__(self, x_in, b_in, dt_raw, seq_total, taps):
        self.rows = x_in.shape[0]
        self.heads = dt_raw.shape[1]
        self.groups = b_in.shape[1] // STATE
        self.per_group = self.heads // self.groups
        self.places = BLOCK // self.rows
        self.blocks = seq_total // self.places
        self.taps = taps
        self.x_blocks = self.per_group * HEAD_DIM // LANES
        self.s_blocks = STATE // LANES
        self.base = self.x_blocks + self.s_blocks
        self.cols = self.base + self.s_blocks
        self.high = self.rows + max(HALO, self.heads)
        self.dt_lanes = slice((self.base - 1) * LANES, self.base * LANES)
        self.halo_rows = -(-self.cols * (taps - 1) // 16) * 16
        self.pad_heads = max(8, self.per_group)
        self.stat_rows = 4 * self.per_group
        self.late = self.places - 1 if self.blocks == 2 else 0
        if self.places != self.groups or self.rows * 2 != LANES or self.places != 4:
            raise ValueError("unsupported shapes")


def lane(start):
    return pl.ds(pl.multiple_of(start, LANES), LANES)


def place_of(sz):
    return lax.rem(lax.axis_index("seq"), sz.places)


def by_partner(own, others, order):
    return [own] + [others[order.index(k)] for k in range(1, len(order) + 1)]


def silu_half(half):
    return half + half * jnp.tanh(half)


def lanes_of(array, group, width):
    return array.at[:, pl.ds(pl.multiple_of(group * width, LANES), width)]


def fetch_all(pairs, sem):
    copies = [pltpu.make_async_copy(source, target, sem.at[i]) for i, (source, target) in enumerate(pairs)]
    for copy in copies:
        copy.start()
    return copies


def c_part(sz, k, m, extra):
    if extra and k in SPLIT:
        return extra[SPLIT.index(k)]
    return m.at[0 : sz.rows, sz.base * LANES :]


def message_parts(sz, group, x, b, c, m, mc):
    rows, wide = sz.rows, sz.x_blocks * LANES
    tail = lanes_of(c, group, STATE).at[rows - HALO :, :]
    return [
        (lanes_of(x, group, wide), m.at[0:rows, 0:wide]),
        (lanes_of(b, group, STATE), m.at[0:rows, wide : sz.base * LANES]),
        (tail, m.at[rows : rows + HALO, 0:STATE]),
        (lanes_of(c, group, STATE), mc),
    ]


def pack_kernel(sz, x, b, c, dt, conv_x, conv_b, conv_c, bias, alog, skip, gain, m0, m1, m2, m3, *rest):
    extra, rest = rest[: len(SPLIT)], rest[len(SPLIT) :]
    late, rest = rest[: sz.late], rest[sz.late :]
    taps_x, taps_b, taps_c, bias_here, alog_here, skip_here, gain_here, dt_here, sem = rest
    place = place_of(sz)
    shared = [
        (dt, dt_here),
        (lanes_of(conv_x, place, sz.x_blocks * LANES), taps_x),
        (lanes_of(conv_b, place, STATE), taps_b),
        (lanes_of(conv_c, place, STATE), taps_c),
        (bias, bias_here),
        (alog, alog_here),
        (skip, skip_here),
        (gain, gain_here),
    ]

    def fill(messages, split):
        pairs = shared[:1]
        for k in (*ORDER, 0):
            m = messages[k]
            part = c_part(sz, k, m, extra if split else None)
            pairs = pairs + message_parts(sz, lax.bitwise_xor(place, k), x, b, c, m, part)
        copies = fetch_all(pairs + shared[1:], sem)
        copies[0].wait()
        here = dt_here[...].astype(F32)
        twice = jnp.concatenate([here, here], axis=1)
        spot = lax.broadcasted_iota(jnp.int32, twice.shape, 1)
        mine = lax.div(spot, sz.rows) == lax.rem(place, 2)
        spread = jnp.where(mine, twice, 0.0).astype(BF16)
        for m in messages:
            m[sz.rows : sz.rows + sz.heads, sz.dt_lanes] = spread
        for copy in copies[1:]:
            copy.wait()

    if sz.late:
        pl.when(in_first(sz))(lambda: fill((m0, m1, m2, m3), True))
        pl.when(in_last(sz))(lambda: fill((m0, *late), False))
    else:
        fill((m0, m1, m2, m3), True)


def conv_block(buffer, count, taps, t):
    n = len(taps)
    first = HALO - (n - 1)
    cols = slice(t * LANES, (t + 1) * LANES)
    total = taps[0] * buffer[first : first + count, cols]
    for i in range(1, n):
        total = total + taps[i] * buffer[first + i : first + i + count, cols]
    return total


def halved_taps(ref, t, n):
    return [0.5 * ref[i : i + 1, t * LANES : (t + 1) * LANES].astype(F32) for i in range(n)]


def gather(sz, buffer, place, base, count, messages):
    for k, m in enumerate(messages):
        source = lax.bitwise_xor(place, k)
        at = pl.ds(pl.multiple_of(HALO + source * sz.rows, 8), sz.rows)
        for t in range(count):
            cols = slice((base + t) * LANES, (base + t + 1) * LANES)
            buffer[at, t * LANES : (t + 1) * LANES] = m[0 : sz.rows, cols].astype(F32)


def of_heads(sz, ref, head0):
    shape = (sz.pad_heads, sz.heads)
    line = lax.broadcasted_iota(jnp.int32, shape, 0)
    spot = lax.broadcasted_iota(jnp.int32, shape, 1)
    row = jnp.broadcast_to(ref[...], shape)
    return jnp.sum(jnp.where(spot == line + head0, row, 0.0), axis=1, keepdims=True)


def convolve(sz, bias, alog, messages, taps_x, taps_b, halo, xc, bc, stats, first, xs, bs, dts):
    chain = sz.blocks > 2
    place = place_of(sz)
    m0, m1, m2, m3 = messages
    dt_at = slice(sz.rows, sz.rows + sz.heads)
    near, far = (
        p[dt_at, sz.dt_lanes].astype(F32) + q[dt_at, sz.dt_lanes].astype(F32)
        for p, q in ((m0, m1), (m2, m3))
    )
    side = lax.div(place, 2)
    dts[:, lane(side * LANES)] = near
    dts[:, lane((1 - side) * LANES)] = far
    head0 = place * sz.per_group
    raw = pltpu.roll(dts[...], lax.rem(sz.heads - head0, sz.heads), 0)[0 : sz.pad_heads]
    raw = raw + of_heads(sz, bias, head0)
    rates = jnp.maximum(raw, 0.0) + jnp.log1p(jnp.exp(-jnp.abs(raw)))
    decays = -jnp.exp(of_heads(sz, alog, head0)) * rates
    high = decays.astype(BF16).astype(F32)
    middle = (decays - high).astype(BF16).astype(F32)
    low = decays - high - middle
    parts = jnp.concatenate([high, middle, low], axis=0).astype(BF16)
    line = lax.broadcasted_iota(jnp.int32, (BLOCK, BLOCK), 0)
    spot = lax.broadcasted_iota(jnp.int32, (BLOCK, BLOCK), 1)
    upto = jnp.where(line <= spot, 1.0, 0.0).astype(BF16)
    sums = dot(parts, upto, NN)
    n = sz.pad_heads
    log_decay = sums[0:n] + sums[n : 2 * n] + sums[2 * n : 3 * n]
    weight = jnp.exp(log_decay[:, BLOCK - 1 : BLOCK] - log_decay) * rates
    g = sz.per_group
    stats[0:g, :] = log_decay[0:g]
    stats[g : 2 * g, :] = rates[0:g]
    stats[2 * g : 3 * g, :] = jnp.exp(log_decay)[0:g]
    stats[3 * g : 4 * g, :] = weight[0:g]
    gather(sz, xs, place, 0, sz.x_blocks, messages)
    gather(sz, bs, place, sz.x_blocks, sz.s_blocks, messages)
    for t in range(sz.base):
        buffer, u = (xs, t) if t < sz.x_blocks else (bs, t - sz.x_blocks)
        cols = slice(u * LANES, (u + 1) * LANES)
        if chain:
            buffer[0:HALO, cols] = halo[t * HALO : (t + 1) * HALO, :]
        else:
            buffer[0:HALO, cols] = jnp.zeros((HALO, LANES), F32)
    for t in range(sz.s_blocks):
        taps = halved_taps(taps_b, t, sz.taps)
        cols = slice(t * LANES, (t + 1) * LANES)
        bc[:, cols] = silu_half(conv_block(bs, BLOCK, taps, t)).astype(BF16)
    for t in range(sz.x_blocks):
        taps = halved_taps(taps_x, t, sz.taps)
        cols = slice(t * LANES, (t + 1) * LANES)
        xc[:, cols] = silu_half(conv_block(xs, BLOCK, taps, t)).astype(BF16)
    for t in range(sz.base):
        buffer, u = (xs, t) if t < sz.x_blocks else (bs, t - sz.x_blocks)
        cols = slice(u * LANES, (u + 1) * LANES)
        first[t * HALO : (t + 1) * HALO, :] = buffer[HALO : 2 * HALO, cols]
    return weight


def in_first(sz):
    return lax.axis_index("seq") < sz.places


def in_last(sz):
    return lax.axis_index("seq") >= (sz.blocks - 1) * sz.places


def state_kernel(sz, bias, alog, m0, ma, mb, mc, taps_x, taps_b, halo,
                 msg, xc, bc, stats, first, xs, bs, dts, tails, packed):
    messages = by_partner(m0, (ma, mb, mc), ORDER)

    def work():
        weight = convolve(sz, bias, alog, messages, taps_x, taps_b, halo, xc, bc, stats, first, xs, bs, dts)
        write_state(sz, messages, weight, msg, xc, bc, xs, bs, tails, packed)

    if not sz.late:
        work()
    else:
        pl.when(jnp.logical_not(in_last(sz)))(work)

        @pl.when(in_last(sz))
        def _():
            msg[...] = jnp.zeros(msg.shape, msg.dtype)


def write_state(sz, messages, weight, msg, xc, bc, xs, bs, tails, packed):
    place = place_of(sz)
    states = []
    for t in range(sz.x_blocks):
        cols = slice(t * LANES, (t + 1) * LANES)
        turned = jnp.transpose(xc[:, cols].astype(F32))
        up = turned[0:HEAD_DIM] * weight[2 * t : 2 * t + 1]
        down = turned[HEAD_DIM:LANES] * weight[2 * t + 1 : 2 * t + 2]
        weighted = jnp.concatenate([up, down], axis=0).astype(BF16)
        states.append(dot(weighted, bc[...], NN))
    for t in range(sz.x_blocks):
        for s in range(sz.s_blocks):
            row = (t * sz.s_blocks + s) * LANES
            part = states[t][:, s * LANES : (s + 1) * LANES]
            msg[row : row + LANES, :] = part.astype(msg.dtype)
    base, over = sz.x_blocks * STATE, sz.taps - 1
    for k, m in enumerate(messages):
        source = lax.bitwise_xor(place, k)
        at = pl.ds(pl.multiple_of(source * HALO, 8), HALO)
        tails[at, :] = m[sz.rows : sz.rows + HALO, 0:STATE].astype(F32)
    packed[...] = jnp.zeros(packed.shape, F32)
    for t in range(sz.cols):
        if t < sz.base:
            buffer, u = (xs, t) if t < sz.x_blocks else (bs, t - sz.x_blocks)
            cols = slice(u * LANES, (u + 1) * LANES)
            last = buffer[BLOCK : BLOCK + HALO, cols]
        else:
            cols = slice((t - sz.base) * LANES, (t - sz.base + 1) * LANES)
            last = tails[(sz.places - 1) * HALO :, cols]
        packed[t * over : (t + 1) * over, :] = last[HALO - over :]
    msg[base:, :] = packed[...].astype(msg.dtype)


def hand_out(sz, total, outs):
    place = place_of(sz)
    for k, o in enumerate(outs):
        target = lax.bitwise_xor(place, k)
        o[...] = total[pl.ds(pl.multiple_of(target * sz.rows, 8), sz.rows), :].astype(BF16)


def inner_kernel(sz, _xc, _bc, _stats, _first, skip, bias, alog, m0, ma, mb, mc, taps_x, taps_b, taps_c, halo, *rest):
    messages = by_partner(m0, (ma, mb, mc), ORDER)
    extra, rest = rest[: len(SPLIT)], rest[len(SPLIT) :]
    late, rest = rest[: sz.late], rest[sz.late :]
    xc, bc, stats, first, *early, out, growth, gains, cc, columns, first_c, cs, turned, xs, bs, dts = rest
    chain = sz.blocks > 2
    place = place_of(sz)

    def gather_c(messages, split):
        parts = [c_part(sz, k, m, extra if split else None) for k, m in enumerate(messages)]
        gather(sz, cs, place, 0, sz.s_blocks, parts)

    if sz.late:
        pl.when(in_first(sz))(lambda: gather_c(messages, True))

        @pl.when(in_last(sz))
        def _():
            late_messages = by_partner(m0, late, ORDER)
            convolve(sz, bias, alog, late_messages, taps_x, taps_b, halo, xc, bc, stats, first, xs, bs, dts)
            gather_c(late_messages, False)
    else:
        gather_c(messages, True)
    g = sz.per_group
    turned[...] = jnp.transpose(stats[...])
    columns[...] = turned[0:EDGE, :]
    skips = of_heads(sz, skip, place * g)
    for t in range(sz.s_blocks):
        cols = slice(t * LANES, (t + 1) * LANES)
        if chain:
            cs[0:HALO, cols] = halo[(sz.base + t) * HALO : (sz.base + t + 1) * HALO, :]
        else:
            cs[0:HALO, cols] = jnp.zeros((HALO, LANES), F32)
        first_c[t * HALO : (t + 1) * HALO, :] = cs[HALO : 2 * HALO, cols]
        taps = halved_taps(taps_c, t, sz.taps)
        cc[:, cols] = silu_half(conv_block(cs, BLOCK, taps, t)).astype(BF16)
    half = BLOCK // 2
    skip_keys = 0 if chain else jnp.where(in_first(sz), 0, EDGE)
    low_lanes = lax.broadcasted_iota(jnp.int32, (half, LANES), 1) < HEAD_DIM
    for t in range(sz.x_blocks):
        cols = slice(t * LANES, (t + 1) * LANES)
        gains[:, cols] = jnp.where(low_lanes[0:8], skips[2 * t : 2 * t + 1], skips[2 * t + 1 : 2 * t + 2])
    for r in range(2):
        width = half * (r + 1)
        at = slice(r * half, (r + 1) * half)
        scores = dot(cc[at, :], bc[0:width, :], NT)
        line = lax.broadcasted_iota(jnp.int32, (half, width), 0) + r * half
        spot = lax.broadcasted_iota(jnp.int32, (half, width), 1)
        keep = (spot <= line) & (spot >= skip_keys)
        for t in range(sz.x_blocks):
            cols = slice(t * LANES, (t + 1) * LANES)
            sums = []
            for h in (2 * t, 2 * t + 1):
                spread = turned[at, h : h + 1] - stats[h : h + 1, 0:width]
                rate = stats[g + h : g + h + 1, 0:width]
                mixing = scores * jnp.exp(jnp.where(keep, spread, -1e30)) * rate
                sums.append(dot(mixing.astype(BF16), xc[0:width, cols], NN))
            both = jnp.where(low_lanes, sums[0], sums[1])
            out[at, cols] = both + gains[0:1, cols] * xc[at, cols].astype(F32)
            rise = 2 * g + 2 * t
            growth[at, cols] = jnp.where(low_lanes, turned[at, rise : rise + 1], turned[at, rise + 1 : rise + 2])
    hand_out(sz, out, early)


def outer_kernel(sz, taps_x, taps_b, taps_c, xc, bc, cc, stats, columns, first, first_c, growth, gains,
                 inner, arrived, o0, o1, o2, o3, edge, ahead, c_all, total):
    chain = sz.blocks > 2
    place = place_of(sz)
    g = sz.per_group
    if chain:
        c_all[...] = cc[...]
    else:
        base = sz.x_blocks * STATE
        renewed, over = [], sz.taps - 1
        ahead[...] = arrived[base:, :].astype(F32)
        for t in range(sz.cols):
            cols = slice(t * LANES, (t + 1) * LANES)
            edge[HALO - over : HALO, cols] = ahead[t * over : (t + 1) * over, :]
            u = t - sz.base
            edge[HALO : 2 * HALO, cols] = (
                first[t * HALO : (t + 1) * HALO, :] if u < 0 else first_c[u * HALO : (u + 1) * HALO, :]
            )
        for t in range(sz.cols):
            which = (t >= sz.x_blocks) + (t >= sz.base)
            u = t - (0, sz.x_blocks, sz.base)[which]
            taps = halved_taps((taps_x, taps_b, taps_c)[which], u, sz.taps)
            fresh = silu_half(conv_block(edge, HALO, taps, t))
            old = (xc, bc, cc)[which][0:EDGE, u * LANES : (u + 1) * LANES].astype(F32)
            renewed.append(jnp.concatenate([fresh, old[HALO:EDGE]], axis=0).astype(BF16))
        for t in range(sz.s_blocks):
            cols = slice(t * LANES, (t + 1) * LANES)
            c_all[EDGE:, cols] = cc[EDGE:, cols]
            c_all[0:EDGE, cols] = renewed[sz.base + t]
        b_edge = jnp.concatenate(renewed[sz.x_blocks : sz.base], axis=1)
        edge_scores = dot(b_edge, c_all[...], NT)
        line = lax.broadcasted_iota(jnp.int32, (EDGE, BLOCK), 0)
        spot = lax.broadcasted_iota(jnp.int32, (EDGE, BLOCK), 1)
        keep = spot >= line
    for t in range(sz.x_blocks):
        cols = slice(t * LANES, (t + 1) * LANES)
        pieces = [
            arrived[(t * sz.s_blocks + s) * LANES : (t * sz.s_blocks + s + 1) * LANES, :]
            for s in range(sz.s_blocks)
        ]
        state = jnp.concatenate(pieces, axis=1)
        out = inner[:, cols] + dot(c_all[...], state, NT) * growth[:, cols]
        if not chain:
            mixed, values = [], []
            edge_low = lax.broadcasted_iota(jnp.int32, (EDGE, LANES), 1) < HEAD_DIM
            x_edge = renewed[t].astype(F32)
            for h in (2 * t, 2 * t + 1):
                spread = stats[h : h + 1, :] - columns[:, h : h + 1]
                rate = columns[:, g + h : g + h + 1]
                mixed.append(edge_scores * jnp.exp(jnp.where(keep, spread, -1e30)) * rate)
                mine = edge_low if h == 2 * t else jnp.logical_not(edge_low)
                values.append(jnp.where(mine, x_edge, 0.0))
            mixed = jnp.concatenate(mixed, axis=0).astype(BF16)
            values = jnp.concatenate(values, axis=0).astype(BF16)
            out = out + dot(mixed, values, TN)
            change = gains[0:1, cols] * (x_edge - xc[0:EDGE, cols].astype(F32))
            total[:, cols] = out
            total[0:EDGE, cols] = out[0:EDGE] + change
        else:
            total[:, cols] = out
    hand_out(sz, total, (o0, o1, o2, o3))


def norm_kernel(sz, o0, ra, rb, rc, e0, ea, eb, ec, z, gain, out, ready, sem):
    place = place_of(sz)
    width = sz.x_blocks * LANES
    copies = []
    early = by_partner(e0, (ea, eb, ec), RETURN)
    for k, part in enumerate(by_partner(o0, (ra, rb, rc), RETURN)):
        at = pl.ds(pl.multiple_of(lax.bitwise_xor(place, k) * width, LANES), width)
        gate = 0.5 * z[:, at].astype(F32)
        value = jnp.where(in_first(sz), early[k][...], part[...]).astype(F32) * silu_half(gate)
        mean = jnp.sum(value * value, axis=-1, keepdims=True) * (1.0 / width)
        ready[k] = (value * lax.rsqrt(mean + 1e-05) * gain[0:1, at]).astype(BF16)
        copies.append(pltpu.make_async_copy(ready.at[k], out.at[:, at], sem.at[k]))
        copies[-1].start()
    for copy in copies:
        copy.wait()


def call(kernel, sz, outs, scratch, specs, flops=0, touched=0, aliases=None, outputs=None):
    return pl.pallas_call(
        functools.partial(kernel, sz),
        out_shape=[jax.ShapeDtypeStruct(s, d) for s, d in outs],
        in_specs=specs,
        out_specs=outputs or [VMEM] * len(outs),
        input_output_aliases=aliases or {},
        scratch_shapes=[s if not isinstance(s, tuple) else pltpu.VMEM(*s) for s in scratch],
        compiler_params=pltpu.CompilerParams(vmem_limit_bytes=24 << 20),
        cost_estimate=pl.CostEstimate(flops=flops, bytes_accessed=touched, transcendentals=0),
    )


def body(x_in, b_in, c_in, z_in, dt_raw, dt_bias, a_log, d_skip, conv_x, conv_b, conv_c, norm_gain):
    seq_total = lax.axis_size("seq")
    sz = Sizes(x_in, b_in, dt_raw, seq_total, conv_x.shape[0])
    n, rows = sz.places, sz.rows
    chain = sz.blocks > 2
    cores = lax.axis_size("head")

    def swap(k, first, end):
        pairs = []
        for i in range(seq_total):
            for core in range(cores):
                there = (i - i % n + ((i % n) ^ k), core) if first <= i < end else (i, cores - 1 - core)
                pairs.append((i * cores + core, there[0] * cores + there[1]))
        return pairs

    def send(array, k, first, end):
        return lax.ppermute(array, ("seq", "head"), swap(k, first, end))

    def onward(k, wrap):
        pairs = [(i, i + n * k) for i in range(seq_total)]
        return [(i, j % seq_total) for i, j in pairs if wrap or j < seq_total]

    def ordered(arrays, order):
        return [arrays[0]] + [arrays[k] for k in order]

    def stay(*arrays):
        return [pltpu.with_memory_space_constraint(a, pltpu.HBM) for a in arrays]

    width = sz.x_blocks * LANES
    vectors = [v.reshape(1, -1) for v in (dt_bias, a_log, d_skip, norm_gain)]
    *sent, taps_x, taps_b, taps_c, bias, alog, skip, gain = call(
        pack_kernel,
        sz,
        [((sz.high, (sz.base + (0 if k in SPLIT else sz.s_blocks)) * LANES), BF16) for k in range(n)]
        + [((rows, STATE), BF16)] * len(SPLIT)
        + [((sz.high, sz.cols * LANES), BF16)] * sz.late
        + [((sz.taps, width), BF16)]
        + [((sz.taps, STATE), BF16)] * 2
        + [((1, sz.heads), F32)] * 3
        + [((1, norm_gain.shape[0]), F32)],
        [((sz.heads, rows), BF16), pltpu.SemaphoreType.DMA((8 + 4 * n,))],
        [HBM] * 11,
    )(*stay(x_in, b_in, c_in, dt_raw.T, conv_x, conv_b, conv_c, *vectors))
    came, split = sent[:n], sent[n : n + len(SPLIT)]
    end = n if sz.late else seq_total
    for k in ORDER:
        came[k] = send(came[k], k, 0, end)
    extra = [send(m, k, 0, end) for m, k in zip(split, SPLIT)]
    late = sent[n + len(SPLIT) :]
    late = [send(late[k - 1], k, n, seq_total) for k in ORDER if sz.late]

    padded = BLOCK + HALO
    edge_rows = sz.halo_rows
    if chain:
        place = lax.rem(lax.axis_index("seq"), n)
        ends = []
        for m in came:
            both = jnp.concatenate([m[rows - HALO : rows, : sz.base * LANES], m[rows : rows + HALO, :STATE]], axis=1)
            ends.append(both.reshape(HALO, sz.cols, LANES).swapaxes(0, 1).reshape(-1, LANES))
        tail = lax.dynamic_index_in_dim(jnp.stack(ends), lax.bitwise_xor(place, n - 1), 0, keepdims=False)
        halo = lax.ppermute(tail, "seq", onward(1, False)).astype(F32)
    else:
        halo = jnp.zeros((8, LANES), F32)

    convolved = [
        ((BLOCK, width), BF16),
        ((BLOCK, STATE), BF16),
        ((sz.stat_rows, BLOCK), F32),
        ((sz.base * HALO, LANES), F32),
    ]
    buffers = [((padded, width), F32), ((padded, STATE), F32), ((sz.heads, BLOCK), F32)]
    msg, *held = call(
        state_kernel,
        sz,
        [((sz.x_blocks * STATE + edge_rows, LANES), F32 if chain else BF16)] + convolved,
        buffers
        + [
            ((n * HALO, STATE), F32),
            ((edge_rows, LANES), F32),
        ],
        [VMEM] * 9,
    )(bias, alog, *ordered(came, ORDER), taps_x, taps_b, halo)

    if chain:
        cut = sz.x_blocks * STATE
        grown = msg[:cut].reshape(sz.x_blocks, sz.s_blocks, 2, HEAD_DIM, LANES)
        fade = jnp.exp(held[2][: sz.per_group, BLOCK - 1]).reshape(sz.x_blocks, 1, 2, 1, 1)
        k = 1
        while k < sz.blocks:
            grown = grown + fade * lax.ppermute(grown, "seq", onward(k, False))
            fade = fade * lax.ppermute(fade, "seq", onward(k, False))
            k *= 2
        msg = jnp.concatenate([grown.reshape(cut, LANES), msg[cut:]], axis=0).astype(BF16)
    arrived = lax.ppermute(msg, "seq", onward(1, True))

    pieces = [((rows, width), BF16)] * n
    xc, bc, stats, first, *early, inner, growth, gains, cc, columns, first_c = call(
        inner_kernel,
        sz,
        convolved
        + pieces
        + [
            ((BLOCK, width), F32),
            ((BLOCK, width), F32),
            ((8, width), F32),
            ((BLOCK, STATE), BF16),
            ((EDGE, sz.stat_rows), F32),
            ((sz.s_blocks * HALO, LANES), F32),
        ],
        [((padded, STATE), F32), ((BLOCK, sz.stat_rows), F32)] + buffers,
        [VMEM] * (15 + len(SPLIT) + sz.late),
        aliases={i: i for i in range(4)},
        flops=1 << 30,
        touched=1 << 22,
    )(*held, skip, bias, alog, *ordered(came, ORDER), taps_x, taps_b, taps_c, halo, *extra, *late)

    for k in RETURN:
        early[k] = send(early[k], k, 0, n)

    back = call(
        outer_kernel,
        sz,
        pieces,
        [
            ((2 * HALO, sz.cols * LANES), F32),
            ((edge_rows, LANES), F32),
            ((BLOCK, STATE), BF16),
            ((BLOCK, width), F32),
        ],
        [VMEM] * 14,
    )(taps_x, taps_b, taps_c, xc, bc, cc, stats, columns, first, first_c, growth, gains, inner, arrived)
    back = list(back)
    for k in RETURN:
        back[k] = send(back[k], k, n, seq_total)

    out = call(
        norm_kernel,
        sz,
        [(x_in.shape, BF16)],
        [((n, rows, width), BF16), pltpu.SemaphoreType.DMA((n,))],
        [VMEM] * 10,
        outputs=[HBM],
    )(
        *ordered(back, RETURN), *ordered(early, RETURN), z_in, gain
    )
    return out[0]


def solution(mesh):
    rows, wide = P(("rep", "seq"), "head"), P(None, "head")
    placed = (rows,) * 5 + (P("head"),) * 3 + (wide,) * 3 + (P("head"),)
    return jax.shard_map(body, mesh=mesh, in_specs=placed, out_specs=rows, check_vma=False)
```

profile of v0, /device:TPU:0, one launch (start us, length us, event | category | flops | bytes accessed | tf_op | source)
XLA Modules:
  0.0 21.8 jit_solution(6392224277672663793)
XLA Ops:
  0.0 1.2 %shard_map.118 = (bf16[72,640]{1,0:T(8,128)(2,1)S(1)}, bf16[72,384]{1,0:T(8,128)(2,1)S(1)}, bf16[72,640]{1,0:T(8,128)(2,1)S(1)}, bf16[72,640]{1,0:T(8,128)(2,1)S...) custom-call(bf16[64,512]{1,0:T(8,128)(2,1)} %x.1, ...), custom_call_target="tpu_custom_call" | custom-call | tf_op jit(solution)/shard_map/pallas_call | solution.py:481
  1.2 3.0 %collective-permute-start.2 = (bf16[72,384]{1,0:T(8,128)(2,1)S(1)}, bf16[72,384]{1,0:T(8,128)(2,1)S(1)}, u32[]{:S(2)}, u32[]{:S(2)}) collective-permute-start(bf16[72,384]{1,0:T(8,128)(2,1)S(1)} %get-tuple-element.51), channel_id=1, source_target_pairs={{0,2},{1,3},{2,0},{3,1},{4,6},{5,7},{6,4},{7,5},{8,9},{9,8},{10,11... | collective-permute-start | bytes 165896 | tf_op jit(solution)/shard_map/ppermute | solution.py:467
  4.2 1.5 %collective-permute-start = (bf16[72,640]{1,0:T(8,128)(2,1)S(1)}, bf16[72,640]{1,0:T(8,128)(2,1)S(1)}, u32[]{:S(2)}, u32[]{:S(2)}) collective-permute-start(bf16[72,640]{1,0:T(8,128)(2,1)S(1)} %get-tuple-element.49), channel_id=1, source_target_pairs={{0,6},{1,7},{2,4},{3,5},{4,2},{5,3},{6,0},{7,1},{8,9},{9,8},{10,11... | collective-permute-start | bytes 276488 | tf_op jit(solution)/shard_map/ppermute | solution.py:467
  5.8 0.0 collective-permute-start.1
  5.8 0.0 collective-permute-start.4
  5.8 0.5 %collective-permute-start.5 = (bf16[72,640]{1,0:T(8,128)(2,1)S(1)}, bf16[72,640]{1,0:T(8,128)(2,1)S(1)}, u32[]{:S(2)}, u32[]{:S(2)}) collective-permute-start(bf16[72,640]{1,0:T(8,128)(2,1)S(1)} %get-tuple-element.59), channel_id=1, source_target_pairs={{0,1},{1,0},{2,3},{3,2},{4,5},{5,4},{6,7},{7,6},{8,12},{9,13},{10,... | collective-permute-start | bytes 276488 | tf_op jit(solution)/shard_map/ppermute | solution.py:467
  6.3 1.0 %collective-permute-done.2.mc = bf16[72,384]{1,0:T(8,128)(2,1)S(1)} collective-permute-done((bf16[72,384]{1,0:T(8,128)(2,1)S(1)}, bf16[72,384]{1,0:T(8,128)(2,1)S(1)}, u32[]{:S(2)}, u32[]{:S(2)}) %collective-permute-start.2) | collective-permute-done | bytes 55328 | tf_op jit(solution)/shard_map/ppermute | solution.py:467
  7.4 0.0 collective-permute-start.6
  7.4 3.2 %collective-permute-done.ma = bf16[72,640]{1,0:T(8,128)(2,1)S(1)} collective-permute-done((bf16[72,640]{1,0:T(8,128)(2,1)S(1)}, bf16[72,640]{1,0:T(8,128)(2,1)S(1)}, u32[]{:S(2)}, u32[]{:S(2)}) %collective-permute-start) | collective-permute-done | bytes 92192 | tf_op jit(solution)/shard_map/ppermute | solution.py:467
  10.6 0.0 collective-permute-start.3
  10.6 0.0 collective-permute-done.1.mb
  10.6 0.7 %shard_map.119 = (bf16[272,128]{1,0:T(8,128)(2,1)S(1)}, bf16[256,128]{1,0:T(8,128)(2,1)S(1)}, bf16[256,256]{1,0:T(8,128)(2,1)S(1)}, f32[8,256]{1,0:T(8,128)S(1)}, f32[24,128]{1,0:T(8,128)S(1)}) custom-call(f32[1,8]{1,0:T(1,128)S(1)} %get-tuple-element.46.bias, f32[1,8]{1,0:T(1,128)S(1)} %get-tuple-element.47.alog, bf16[72,640]{1,0:T(8,128)(2,1)S(1)} %get-tuple-element.48.m0, ...), custom_call_target="tpu_custom_call" | custom-call | tf_op jit(solution)/shard_map/pallas_call | solution.py:522
  11.2 0.1 collective-permute-start.7
  11.3 3.2 %collective-permute-done.3.rest_0_ = bf16[64,256]{1,0:T(8,128)(2,1)S(1)} collective-permute-done((bf16[64,256]{1,0:T(8,128)(2,1)S(1)}, bf16[64,256]{1,0:T(8,128)(2,1)S(1)}, u32[]{:S(2)}, u32[]{:S(2)}) %collective-permute-start.3) | collective-permute-done | bytes 32800 | tf_op jit(solution)/shard_map/ppermute | solution.py:467
  14.5 0.0 collective-permute-done.4.rest_1_
  14.5 0.0 collective-permute-done.5.rest_2_
  14.5 0.0 collective-permute-done.6.rest_3_
  14.5 0.6 %shard_map.120 = (bf16[256,128]{1,0:T(8,128)(2,1)S(1)}, bf16[256,256]{1,0:T(8,128)(2,1)S(1)}, f32[8,256]{1,0:T(8,128)S(1)}, f32[24,128]{1,0:T(8,128)S(1)}, bf16[...) custom-call(bf16[256,128]{1,0:T(8,128)(2,1)S(1)} %get-tuple-element., ...), custom_call_target="tpu_custom_call", output_to_operand_aliasing={{0}: (0, {}), {1}: (1, {}), {2}: (2, {}), {3}: (3, {})} | custom-call | flops 1073741824 | bytes 4194304 | tf_op jit(solution)/shard_map/pallas_call | solution.py:547
  15.1 1.3 %collective-permute-start.11 = (bf16[64,128]{1,0:T(8,128)(2,1)S(1)}, bf16[64,128]{1,0:T(8,128)(2,1)S(1)}, u32[]{:S(2)}, u32[]{:S(2)}) collective-permute-start(bf16[64,128]{1,0:T(8,128)(2,1)S(1)} %get-tuple-element.77), channel_id=1, source_target_pairs={{0,6},{1,7},{2,4},{3,5},{4,2},{5,3},{6,0},{7,1},{8,9},{9,8},{10,11... | collective-permute-start | bytes 49160 | tf_op jit(solution)/shard_map/ppermute | solution.py:467
  16.5 0.2 collective-permute-start.12
  16.7 2.0 %collective-permute-start.13 = (bf16[64,128]{1,0:T(8,128)(2,1)S(1)}, bf16[64,128]{1,0:T(8,128)(2,1)S(1)}, u32[]{:S(2)}, u32[]{:S(2)}) collective-permute-start(bf16[64,128]{1,0:T(8,128)(2,1)S(1)} %get-tuple-element.79), channel_id=1, source_target_pairs={{0,2},{1,3},{2,0},{3,1},{4,6},{5,7},{6,4},{7,5},{8,9},{9,8},{10,11... | collective-permute-start | bytes 49160 | tf_op jit(solution)/shard_map/ppermute | solution.py:467
  18.7 0.0 collective-permute-done.7.arrived
  18.7 0.4 %shard_map.121 = (bf16[64,128]{1,0:T(8,128)(2,1)S(1)}, bf16[64,128]{1,0:T(8,128)(2,1)S(1)}, bf16[64,128]{1,0:T(8,128)(2,1)S(1)}, bf16[64,128]{1,0:T(8,128)(2,1)S(1)}) custom-call(bf16[4,128]{1,0:T(4,128)(2,1)S(1)} %get-tuple-element.43.taps_x, bf16[4,256]{1,0:T(4,128)(2,1)S(1)} %get-tuple-element.44.taps_b, bf16[4,256]{1,0:T(4,128)(2,1)S(1)} %get-tuple-element.45.taps_c, ...), custom_call_target="tpu_custom_call" | custom-call | tf_op jit(solution)/shard_map/pallas_call | solution.py:570
  19.1 0.1 collective-permute-start.8
  19.2 0.5 %collective-permute-start.9 = (bf16[64,128]{1,0:T(8,128)(2,1)S(1)}, bf16[64,128]{1,0:T(8,128)(2,1)S(1)}, u32[]{:S(2)}, u32[]{:S(2)}) collective-permute-start(bf16[64,128]{1,0:T(8,128)(2,1)S(1)} %get-tuple-element.74), channel_id=1, source_target_pairs={{0,1},{1,0},{2,3},{3,2},{4,5},{5,4},{6,7},{7,6},{8,12},{9,13},{10,... | collective-permute-start | bytes 49160 | tf_op jit(solution)/shard_map/ppermute | solution.py:467
  19.7 0.1 collective-permute-done.11.ea
  19.8 0.0 collective-permute-start.10
  19.8 0.4 %collective-permute-done.12.eb = bf16[64,128]{1,0:T(8,128)(2,1)S(1)} collective-permute-done((bf16[64,128]{1,0:T(8,128)(2,1)S(1)}, bf16[64,128]{1,0:T(8,128)(2,1)S(1)}, u32[]{:S(2)}, u32[]{:S(2)}) %collective-permute-start.12) | collective-permute-done | bytes 16416 | tf_op jit(solution)/shard_map/ppermute | solution.py:467
  20.2 0.2 collective-permute-done.13.ec
  20.4 0.2 collective-permute-done.9.rb
  20.6 0.5 %collective-permute-done.10.rc = bf16[64,128]{1,0:T(8,128)(2,1)S(1)} collective-permute-done((bf16[64,128]{1,0:T(8,128)(2,1)S(1)}, bf16[64,128]{1,0:T(8,128)(2,1)S(1)}, u32[]{:S(2)}, u32[]{:S(2)}) %collective-permute-start.10) | collective-permute-done | bytes 16416 | tf_op jit(solution)/shard_map/ppermute | solution.py:467
  21.0 0.8 %shard_map.122 = bf16[64,512]{1,0:T(8,128)(2,1)} custom-call(bf16[64,128]{1,0:T(8,128)(2,1)S(1)} %get-tuple-element.72.o0, bf16[64,128]{1,0:T(8,128)(2,1)S(1)} %collective-permute-done.8.ra, bf16[64,128]{1,0:T(8,128)(2,1)S(1)} %collective-permute-done.9.rb, bf16[64,128]{1,0:T(8,128)(2,1)S(1)} %collective-permute-done.10.rc, ...), custom_call_target="tpu_custom_call" | custom-call | tf_op jit(solution)/shard_map/pallas_call | solution.py:586
  (4 shorter events, 0.0 us)
Async XLA Ops:
  1.2 6.2 %collective-permute-start.2 = (bf16[72,384]{1,0:T(8,128)(2,1)S(1)}, bf16[72,384]{1,0:T(8,128)(2,1)S(1)}, u32[]{:S(2)}, u32[]{:S(2)}) collective-permute-start(bf16[72,384]{1,0:T(8,128)(2,1)S(1)} %get-tuple-element.51), channel_id=1, source_target_pairs={{0,2},{1,3},{2,0},{3,1},{4,6},{5,7},{6,4},{7,5},{8,9},{9,8},{10,11... | collective-permute-start | bytes 165896 | tf_op jit(solution)/shard_map/ppermute | solution.py:467
  4.2 6.3 %collective-permute-start = (bf16[72,640]{1,0:T(8,128)(2,1)S(1)}, bf16[72,640]{1,0:T(8,128)(2,1)S(1)}, u32[]{:S(2)}, u32[]{:S(2)}) collective-permute-start(bf16[72,640]{1,0:T(8,128)(2,1)S(1)} %get-tuple-element.49), channel_id=1, source_target_pairs={{0,6},{1,7},{2,4},{3,5},{4,2},{5,3},{6,0},{7,1},{8,9},{9,8},{10,11... | collective-permute-start | bytes 276488 | tf_op jit(solution)/shard_map/ppermute | solution.py:467
  5.8 4.8 %collective-permute-start.1 = (bf16[72,640]{1,0:T(8,128)(2,1)S(1)}, bf16[72,640]{1,0:T(8,128)(2,1)S(1)}, u32[]{:S(2)}, u32[]{:S(2)}) collective-permute-start(bf16[72,640]{1,0:T(8,128)(2,1)S(1)} %get-tuple-element.50), channel_id=1, source_target_pairs={{0,4},{1,5},{2,6},{3,7},{4,0},{5,1},{6,2},{7,3},{8,9},{9,8},{10,11... | collective-permute-start | bytes 276488 | tf_op jit(solution)/shard_map/ppermute | solution.py:467
  5.8 8.7 %collective-permute-start.4 = (bf16[72,640]{1,0:T(8,128)(2,1)S(1)}, bf16[72,640]{1,0:T(8,128)(2,1)S(1)}, u32[]{:S(2)}, u32[]{:S(2)}) collective-permute-start(bf16[72,640]{1,0:T(8,128)(2,1)S(1)} %get-tuple-element.58), channel_id=1, source_target_pairs={{0,1},{1,0},{2,3},{3,2},{4,5},{5,4},{6,7},{7,6},{8,14},{9,15},{10,... | collective-permute-start | bytes 276488 | tf_op jit(solution)/shard_map/ppermute | solution.py:467
  5.8 8.7 %collective-permute-start.5 = (bf16[72,640]{1,0:T(8,128)(2,1)S(1)}, bf16[72,640]{1,0:T(8,128)(2,1)S(1)}, u32[]{:S(2)}, u32[]{:S(2)}) collective-permute-start(bf16[72,640]{1,0:T(8,128)(2,1)S(1)} %get-tuple-element.59), channel_id=1, source_target_pairs={{0,1},{1,0},{2,3},{3,2},{4,5},{5,4},{6,7},{7,6},{8,12},{9,13},{10,... | collective-permute-start | bytes 276488 | tf_op jit(solution)/shard_map/ppermute | solution.py:467
  7.4 7.1 %collective-permute-start.6 = (bf16[72,640]{1,0:T(8,128)(2,1)S(1)}, bf16[72,640]{1,0:T(8,128)(2,1)S(1)}, u32[]{:S(2)}, u32[]{:S(2)}) collective-permute-start(bf16[72,640]{1,0:T(8,128)(2,1)S(1)} %get-tuple-element.60), channel_id=1, source_target_pairs={{0,1},{1,0},{2,3},{3,2},{4,5},{5,4},{6,7},{7,6},{8,10},{9,11},{10,... | collective-permute-start | bytes 276488 | tf_op jit(solution)/shard_map/ppermute | solution.py:467
  10.6 3.9 %collective-permute-start.3 = (bf16[64,256]{1,0:T(8,128)(2,1)S(1)}, bf16[64,256]{1,0:T(8,128)(2,1)S(1)}, u32[]{:S(2)}, u32[]{:S(2)}) collective-permute-start(bf16[64,256]{1,0:T(8,128)(2,1)S(1)} %get-tuple-element.57), channel_id=1, source_target_pairs={{0,2},{1,3},{2,0},{3,1},{4,6},{5,7},{6,4},{7,5},{8,9},{9,8},{10,11... | collective-permute-start | bytes 98312 | tf_op jit(solution)/shard_map/ppermute | solution.py:467
  11.2 7.5 %collective-permute-start.7 = (bf16[272,128]{1,0:T(8,128)(2,1)S(1)}, bf16[272,128]{1,0:T(8,128)(2,1)S(1)}, u32[]{:S(2)}, u32[]{:S(2)}) collective-permute-start(bf16[272,128]{1,0:T(8,128)(2,1)S(1)} %get-tuple-element.71), channel_id=1, source_target_pairs={{0,8},{2,10},{4,12},{6,14},{8,0},{10,2},{12,4},{14,6},{1,9},{3,11}... | collective-permute-start | bytes 208904 | tf_op jit(solution)/shard_map/ppermute | solution.py:544
  15.1 4.7 %collective-permute-start.11 = (bf16[64,128]{1,0:T(8,128)(2,1)S(1)}, bf16[64,128]{1,0:T(8,128)(2,1)S(1)}, u32[]{:S(2)}, u32[]{:S(2)}) collective-permute-start(bf16[64,128]{1,0:T(8,128)(2,1)S(1)} %get-tuple-element.77), channel_id=1, source_target_pairs={{0,6},{1,7},{2,4},{3,5},{4,2},{5,3},{6,0},{7,1},{8,9},{9,8},{10,11... | collective-permute-start | bytes 49160 | tf_op jit(solution)/shard_map/ppermute | solution.py:467
  16.5 3.7 %collective-permute-start.12 = (bf16[64,128]{1,0:T(8,128)(2,1)S(1)}, bf16[64,128]{1,0:T(8,128)(2,1)S(1)}, u32[]{:S(2)}, u32[]{:S(2)}) collective-permute-start(bf16[64,128]{1,0:T(8,128)(2,1)S(1)} %get-tuple-element.78), channel_id=1, source_target_pairs={{0,4},{1,5},{2,6},{3,7},{4,0},{5,1},{6,2},{7,3},{8,9},{9,8},{10,11... | collective-permute-start | bytes 49160 | tf_op jit(solution)/shard_map/ppermute | solution.py:467
  16.7 3.7 %collective-permute-start.13 = (bf16[64,128]{1,0:T(8,128)(2,1)S(1)}, bf16[64,128]{1,0:T(8,128)(2,1)S(1)}, u32[]{:S(2)}, u32[]{:S(2)}) collective-permute-start(bf16[64,128]{1,0:T(8,128)(2,1)S(1)} %get-tuple-element.79), channel_id=1, source_target_pairs={{0,2},{1,3},{2,0},{3,1},{4,6},{5,7},{6,4},{7,5},{8,9},{9,8},{10,11... | collective-permute-start | bytes 49160 | tf_op jit(solution)/shard_map/ppermute | solution.py:467
  18.7 2.3 %copy-start = (bf16[64,512]{1,0:T(8,128)(2,1)S(1)}, bf16[64,512]{1,0:T(8,128)(2,1)}, u32[]{:S(2)}) copy-start(bf16[64,512]{1,0:T(8,128)(2,1)} %z.1) | copy-start | bytes 196612
  19.1 1.3 %collective-permute-start.8 = (bf16[64,128]{1,0:T(8,128)(2,1)S(1)}, bf16[64,128]{1,0:T(8,128)(2,1)S(1)}, u32[]{:S(2)}, u32[]{:S(2)}) collective-permute-start(bf16[64,128]{1,0:T(8,128)(2,1)S(1)} %get-tuple-element.73), channel_id=1, source_target_pairs={{0,1},{1,0},{2,3},{3,2},{4,5},{5,4},{6,7},{7,6},{8,14},{9,15},{10,... | collective-permute-start | bytes 49160 | tf_op jit(solution)/shard_map/ppermute | solution.py:467
  19.2 1.3 %collective-permute-start.9 = (bf16[64,128]{1,0:T(8,128)(2,1)S(1)}, bf16[64,128]{1,0:T(8,128)(2,1)S(1)}, u32[]{:S(2)}, u32[]{:S(2)}) collective-permute-start(bf16[64,128]{1,0:T(8,128)(2,1)S(1)} %get-tuple-element.74), channel_id=1, source_target_pairs={{0,1},{1,0},{2,3},{3,2},{4,5},{5,4},{6,7},{7,6},{8,12},{9,13},{10,... | collective-permute-start | bytes 49160 | tf_op jit(solution)/shard_map/ppermute | solution.py:467
  19.8 1.2 %collective-permute-start.10 = (bf16[64,128]{1,0:T(8,128)(2,1)S(1)}, bf16[64,128]{1,0:T(8,128)(2,1)S(1)}, u32[]{:S(2)}, u32[]{:S(2)}) collective-permute-start(bf16[64,128]{1,0:T(8,128)(2,1)S(1)} %get-tuple-element.75), channel_id=1, source_target_pairs={{0,1},{1,0},{2,3},{3,2},{4,5},{5,4},{6,7},{7,6},{8,10},{9,11},{10,... | collective-permute-start | bytes 49160 | tf_op jit(solution)/shard_map/ppermute | solution.py:467
where the time goes:
time: 22 us; the launch traced here: 21.8 us
  starting transfers between devices  9.32 us (42%)
  waiting for transfers between devices  8.7 us (40%)
  Pallas kernels  3.7 us (17%)
    ppermute x13, starting transfers between devices, send(): return lax.ppermute(array, ('seq', 'head'), swap(k, first, end))  9.25 us
    ppermute x13, waiting for transfers between devices, send(): return lax.ppermute(array, ('seq', 'head'), swap(k, first, end))  8.69 us
    pallas_call x1, Pallas kernels, body(): call(pack_kernel, sz, [((sz.high, (sz.base + (0 if k in SPLIT else sz.s_b...  1.19 us
    pallas_call x1, Pallas kernels, body(): call(norm_kernel, sz, [(x_in.shape, BF16)], [((n, rows, width), BF16), pl...  0.78 us
    pallas_call x1, Pallas kernels, body(): call(state_kernel, sz, [((sz.x_blocks * STATE + edge_rows, LANES), F32 if...  0.65 us
    pallas_call x1, Pallas kernels, body(): call(inner_kernel, sz, convolved + pieces + [((BLOCK, width), F32), ((BLO...  0.64 us
    pallas_call x1, Pallas kernels, body(): call(outer_kernel, sz, pieces, [((2 * HALO, sz.cols * LANES), F32), ((edg...  0.45 us
  transfers between devices with their start and end apart: 14, of which 8 were waited for; matrix products, arithmetic and copies ran while one was open for 0% of the time, Pallas kernels for 8%

commit v1 on v0

--- a/solution.py
+++ b/solution.py
@@ -43,8 +43,6 @@
         self.s_blocks = STATE // LANES
         self.base = self.x_blocks + self.s_blocks
         self.cols = self.base + self.s_blocks
-        self.high = self.rows + max(HALO, self.heads)
-        self.dt_lanes = slice((self.base - 1) * LANES, self.base * LANES)
         self.halo_rows = -(-self.cols * (taps - 1) // 16) * 16
         self.pad_heads = max(8, self.per_group)
         self.stat_rows = 4 * self.per_group
@@ -73,6 +71,19 @@
     return array.at[:, pl.ds(pl.multiple_of(group * width, LANES), width)]
 
 
+def layout(sz, k, apart):
+    c_high = HALO if apart and k in SPLIT else sz.rows
+    starts = [t * sz.rows for t in range(sz.base)] + [sz.base * sz.rows + u * c_high for u in range(sz.s_blocks)]
+    end = starts[-1] + c_high
+    return starts, end, end + sz.heads
+
+
+def tail_rows(sz, k, t):
+    starts, _, _ = layout(sz, k, True)
+    last = starts[t] + (HALO if t >= sz.base and k in SPLIT else sz.rows)
+    return slice(last - HALO, last)
+
+
 def fetch_all(pairs, sem):
     copies = [pltpu.make_async_copy(source, target, sem.at[i]) for i, (source, target) in enumerate(pairs)]
     for copy in copies:
@@ -80,21 +91,21 @@
     return copies
 
 
-def c_part(sz, k, m, extra):
-    if extra and k in SPLIT:
-        return extra[SPLIT.index(k)]
-    return m.at[0 : sz.rows, sz.base * LANES :]
-
-
-def message_parts(sz, group, x, b, c, m, mc):
-    rows, wide = sz.rows, sz.x_blocks * LANES
-    tail = lanes_of(c, group, STATE).at[rows - HALO :, :]
-    return [
-        (lanes_of(x, group, wide), m.at[0:rows, 0:wide]),
-        (lanes_of(b, group, STATE), m.at[0:rows, wide : sz.base * LANES]),
-        (tail, m.at[rows : rows + HALO, 0:STATE]),
-        (lanes_of(c, group, STATE), mc),
-    ]
+def message_parts(sz, k, group, x, b, c, m, extra):
+    rows, apart = sz.rows, extra is not None
+    starts, _, _ = layout(sz, k, apart)
+    pairs = []
+    for t in range(sz.cols):
+        which = (t >= sz.x_blocks) + (t >= sz.base)
+        u = t - (0, sz.x_blocks, sz.base)[which]
+        first = group * (sz.x_blocks, sz.s_blocks, sz.s_blocks)[which] + u
+        source = (x, b, c)[which].at[:, lane(first * LANES)]
+        if which == 2 and apart and k in SPLIT:
+            pairs.append((source, extra[SPLIT.index(k)].at[u * rows : (u + 1) * rows, :]))
+            pairs.append((source.at[rows - HALO :, :], m.at[starts[t] : starts[t] + HALO, :]))
+        else:
+            pairs.append((source, m.at[starts[t] : starts[t] + rows, :]))
+    return pairs
 
 
 def pack_kernel(sz, x, b, c, dt, conv_x, conv_b, conv_c, bias, alog, skip, gain, m0, m1, m2, m3, *rest):
@@ -117,8 +128,8 @@
         pairs = shared[:1]
         for k in (*ORDER, 0):
             m = messages[k]
-            part = c_part(sz, k, m, extra if split else None)
-            pairs = pairs + message_parts(sz, lax.bitwise_xor(place, k), x, b, c, m, part)
+            group = lax.bitwise_xor(place, k)
+            pairs = pairs + message_parts(sz, k, group, x, b, c, m, extra if split else None)
         copies = fetch_all(pairs + shared[1:], sem)
         copies[0].wait()
         here = dt_here[...].astype(F32)
@@ -126,8 +137,8 @@
         spot = lax.broadcasted_iota(jnp.int32, twice.shape, 1)
         mine = lax.div(spot, sz.rows) == lax.rem(place, 2)
         spread = jnp.where(mine, twice, 0.0).astype(BF16)
-        for m in messages:
-            m[sz.rows : sz.rows + sz.heads, sz.dt_lanes] = spread
+        for k, m in enumerate(messages):
+            m[layout(sz, k, split)[1] :, :] = spread
         for copy in copies[1:]:
             copy.wait()
 
@@ -152,13 +163,12 @@
     return [0.5 * ref[i : i + 1, t * LANES : (t + 1) * LANES].astype(F32) for i in range(n)]
 
 
-def gather(sz, buffer, place, base, count, messages):
+def gather(sz, buffer, place, messages, starts):
     for k, m in enumerate(messages):
         source = lax.bitwise_xor(place, k)
         at = pl.ds(pl.multiple_of(HALO + source * sz.rows, 8), sz.rows)
-        for t in range(count):
-            cols = slice((base + t) * LANES, (base + t + 1) * LANES)
-            buffer[at, t * LANES : (t + 1) * LANES] = m[0 : sz.rows, cols].astype(F32)
+        for t, row in enumerate(starts[k]):
+            buffer[at, t * LANES : (t + 1) * LANES] = m[row : row + sz.rows, :].astype(F32)
 
 
 def of_heads(sz, ref, head0):
@@ -169,15 +179,12 @@
     return jnp.sum(jnp.where(spot == line + head0, row, 0.0), axis=1, keepdims=True)
 
 
-def convolve(sz, bias, alog, messages, taps_x, taps_b, halo, xc, bc, stats, first, xs, bs, dts):
+def convolve(sz, bias, alog, messages, taps_x, taps_b, halo, xc, bc, stats, first, xs, bs, dts, apart):
     chain = sz.blocks > 2
     place = place_of(sz)
-    m0, m1, m2, m3 = messages
-    dt_at = slice(sz.rows, sz.rows + sz.heads)
-    near, far = (
-        p[dt_at, sz.dt_lanes].astype(F32) + q[dt_at, sz.dt_lanes].astype(F32)
-        for p, q in ((m0, m1), (m2, m3))
-    )
+    places = [layout(sz, k, apart) for k in range(sz.places)]
+    logits = [m[at[1] :, :].astype(F32) for m, at in zip(messages, places)]
+    near, far = logits[0] + logits[1], logits[2] + logits[3]
     side = lax.div(place, 2)
     dts[:, lane(side * LANES)] = near
     dts[:, lane((1 - side) * LANES)] = far
@@ -202,8 +209,8 @@
     stats[g : 2 * g, :] = rates[0:g]
     stats[2 * g : 3 * g, :] = jnp.exp(log_decay)[0:g]
     stats[3 * g : 4 * g, :] = weight[0:g]
-    gather(sz, xs, place, 0, sz.x_blocks, messages)
-    gather(sz, bs, place, sz.x_blocks, sz.s_blocks, messages)
+    gather(sz, xs, place, messages, [at[0][: sz.x_blocks] for at in places])
+    gather(sz, bs, place, messages, [at[0][sz.x_blocks : sz.base] for at in places])
     for t in range(sz.base):
         buffer, u = (xs, t) if t < sz.x_blocks else (bs, t - sz.x_blocks)
         cols = slice(u * LANES, (u + 1) * LANES)
@@ -239,7 +246,7 @@
     messages = by_partner(m0, (ma, mb, mc), ORDER)
 
     def work():
-        weight = convolve(sz, bias, alog, messages, taps_x, taps_b, halo, xc, bc, stats, first, xs, bs, dts)
+        weight = convolve(sz, bias, alog, messages, taps_x, taps_b, halo, xc, bc, stats, first, xs, bs, dts, True)
         write_state(sz, messages, weight, msg, xc, bc, xs, bs, tails, packed)
 
     if not sz.late:
@@ -271,7 +278,8 @@
     for k, m in enumerate(messages):
         source = lax.bitwise_xor(place, k)
         at = pl.ds(pl.multiple_of(source * HALO, 8), HALO)
-        tails[at, :] = m[sz.rows : sz.rows + HALO, 0:STATE].astype(F32)
+        for u in range(sz.s_blocks):
+            tails[at, u * LANES : (u + 1) * LANES] = m[tail_rows(sz, k, sz.base + u), :].astype(F32)
     packed[...] = jnp.zeros(packed.shape, F32)
     for t in range(sz.cols):
         if t < sz.base:
@@ -301,8 +309,12 @@
     place = place_of(sz)
 
     def gather_c(messages, split):
-        parts = [c_part(sz, k, m, extra if split else None) for k, m in enumerate(messages)]
-        gather(sz, cs, place, 0, sz.s_blocks, parts)
+        parts, starts = [], []
+        for k, m in enumerate(messages):
+            apart = split and k in SPLIT
+            parts.append(extra[SPLIT.index(k)] if apart else m)
+            starts.append([u * sz.rows for u in range(sz.s_blocks)] if apart else layout(sz, k, False)[0][sz.base :])
+        gather(sz, cs, place, parts, starts)
 
     if sz.late:
         pl.when(in_first(sz))(lambda: gather_c(messages, True))
@@ -310,7 +322,7 @@
         @pl.when(in_last(sz))
         def _():
             late_messages = by_partner(m0, late, ORDER)
-            convolve(sz, bias, alog, late_messages, taps_x, taps_b, halo, xc, bc, stats, first, xs, bs, dts)
+            convolve(sz, bias, alog, late_messages, taps_x, taps_b, halo, xc, bc, stats, first, xs, bs, dts, False)
             gather_c(late_messages, False)
     else:
         gather_c(messages, True)
@@ -481,14 +493,14 @@
     *sent, taps_x, taps_b, taps_c, bias, alog, skip, gain = call(
         pack_kernel,
         sz,
-        [((sz.high, (sz.base + (0 if k in SPLIT else sz.s_blocks)) * LANES), BF16) for k in range(n)]
-        + [((rows, STATE), BF16)] * len(SPLIT)
-        + [((sz.high, sz.cols * LANES), BF16)] * sz.late
+        [((layout(sz, k, True)[2], LANES), BF16) for k in range(n)]
+        + [((sz.s_blocks * rows, LANES), BF16)] * len(SPLIT)
+        + [((layout(sz, 0, False)[2], LANES), BF16)] * sz.late
         + [((sz.taps, width), BF16)]
         + [((sz.taps, STATE), BF16)] * 2
         + [((1, sz.heads), F32)] * 3
         + [((1, norm_gain.shape[0]), F32)],
-        [((sz.heads, rows), BF16), pltpu.SemaphoreType.DMA((8 + 4 * n,))],
+        [((sz.heads, rows), BF16), pltpu.SemaphoreType.DMA((8 + (sz.cols + sz.s_blocks) * n,))],
         [HBM] * 11,
     )(*stay(x_in, b_in, c_in, dt_raw.T, conv_x, conv_b, conv_c, *vectors))
     came, split = sent[:n], sent[n : n + len(SPLIT)]
@@ -504,9 +516,8 @@
     if chain:
         place = lax.rem(lax.axis_index("seq"), n)
         ends = []
-        for m in came:
-            both = jnp.concatenate([m[rows - HALO : rows, : sz.base * LANES], m[rows : rows + HALO, :STATE]], axis=1)
-            ends.append(both.reshape(HALO, sz.cols, LANES).swapaxes(0, 1).reshape(-1, LANES))
+        for k, m in enumerate(came):
+            ends.append(jnp.concatenate([m[tail_rows(sz, k, t)] for t in range(sz.cols)], axis=0))
         tail = lax.dynamic_index_in_dim(jnp.stack(ends), lax.bitwise_xor(place, n - 1), 0, keepdims=False)
         halo = lax.ppermute(tail, "seq", onward(1, False)).astype(F32)
     else:

time: 22 us -> 21.9 us (level)
  no operation moved by 1% of the time
where the time goes in v1:
time: 21.9 us; the launch traced here: 21.7 us
  starting transfers between devices  9.32 us (43%)
  waiting for transfers between devices  8.52 us (39%)
  Pallas kernels  3.78 us (17%)
    ppermute x13, starting transfers between devices, send(): return lax.ppermute(array, ('seq', 'head'), swap(k, first, end))  9.25 us
    ppermute x13, waiting for transfers between devices, send(): return lax.ppermute(array, ('seq', 'head'), swap(k, first, end))  8.52 us
    pallas_call x1, Pallas kernels, body(): call(pack_kernel, sz, [((layout(sz, k, True)[2], LANES), BF16) for k in r...  1.27 us
    pallas_call x1, Pallas kernels, body(): call(norm_kernel, sz, [(x_in.shape, BF16)], [((n, rows, width), BF16), pl...  0.78 us
    pallas_call x1, Pallas kernels, body(): call(state_kernel, sz, [((sz.x_blocks * STATE + edge_rows, LANES), F32 if...  0.65 us
    pallas_call x1, Pallas kernels, body(): call(inner_kernel, sz, convolved + pieces + [((BLOCK, width), F32), ((BLO...  0.64 us
    pallas_call x1, Pallas kernels, body(): call(outer_kernel, sz, pieces, [((2 * HALO, sz.cols * LANES), F32), ((edg...  0.44 us
  transfers between devices with their start and end apart: 14, of which 8 were waited for; matrix products, arithmetic and copies ran while one was open for 0% of the time, Pallas kernels for 8%

profile of v1, /device:TPU:0, one launch (start us, length us, event | category | flops | bytes accessed | tf_op | source)
XLA Modules:
  0.0 21.7 jit_solution(15732305555200882662)
XLA Ops:
  0.0 1.3 %shard_map.118 = (bf16[328,128]{1,0:T(8,128)(2,1)S(1)}, bf16[216,128]{1,0:T(8,128)(2,1)S(1)}, bf16[328,128]{1,0:T(8,128)(2,1)S(1)}, bf16[328,128]{1,0:T(8,128)(2...) custom-call(bf16[64,512]{1,0:T(8,128)(2,1)} %x.1, ...), custom_call_target="tpu_custom_call" | custom-call | tf_op jit(solution)/shard_map/pallas_call | solution.py:493
  1.3 3.0 %collective-permute-start.2 = (bf16[216,128]{1,0:T(8,128)(2,1)S(1)}, bf16[216,128]{1,0:T(8,128)(2,1)S(1)}, u32[]{:S(2)}, u32[]{:S(2)}) collective-permute-start(bf16[216,128]{1,0:T(8,128)(2,1)S(1)} %get-tuple-element.51), channel_id=1, source_target_pairs={{0,2},{1,3},{2,0},{3,1},{4,6},{5,7},{6,4},{7,5},{8,9},{9,8},{10,11... | collective-permute-start | bytes 165896 | tf_op jit(solution)/shard_map/ppermute | solution.py:479
  4.3 1.5 %collective-permute-start = (bf16[328,128]{1,0:T(8,128)(2,1)S(1)}, bf16[328,128]{1,0:T(8,128)(2,1)S(1)}, u32[]{:S(2)}, u32[]{:S(2)}) collective-permute-start(bf16[328,128]{1,0:T(8,128)(2,1)S(1)} %get-tuple-element.49), channel_id=1, source_target_pairs={{0,6},{1,7},{2,4},{3,5},{4,2},{5,3},{6,0},{7,1},{8,9},{9,8},{10,11... | collective-permute-start | bytes 251912 | tf_op jit(solution)/shard_map/ppermute | solution.py:479
  5.9 0.0 collective-permute-start.1
  5.9 0.0 collective-permute-start.4
  5.9 0.5 %collective-permute-start.5 = (bf16[328,128]{1,0:T(8,128)(2,1)S(1)}, bf16[328,128]{1,0:T(8,128)(2,1)S(1)}, u32[]{:S(2)}, u32[]{:S(2)}) collective-permute-start(bf16[328,128]{1,0:T(8,128)(2,1)S(1)} %get-tuple-element.59), channel_id=1, source_target_pairs={{0,1},{1,0},{2,3},{3,2},{4,5},{5,4},{6,7},{7,6},{8,12},{9,13},{10,... | collective-permute-start | bytes 251912 | tf_op jit(solution)/shard_map/ppermute | solution.py:479
  6.4 0.9 %collective-permute-done.2.mc = bf16[216,128]{1,0:T(8,128)(2,1)S(1)} collective-permute-done((bf16[216,128]{1,0:T(8,128)(2,1)S(1)}, bf16[216,128]{1,0:T(8,128)(2,1)S(1)}, u32[]{:S(2)}, u32[]{:S(2)}) %collective-permute-start.2) | collective-permute-done | bytes 55328 | tf_op jit(solution)/shard_map/ppermute | solution.py:479
  7.3 0.0 collective-permute-start.6
  7.3 3.2 %collective-permute-done.ma = bf16[328,128]{1,0:T(8,128)(2,1)S(1)} collective-permute-done((bf16[328,128]{1,0:T(8,128)(2,1)S(1)}, bf16[328,128]{1,0:T(8,128)(2,1)S(1)}, u32[]{:S(2)}, u32[]{:S(2)}) %collective-permute-start) | collective-permute-done | bytes 84000 | tf_op jit(solution)/shard_map/ppermute | solution.py:479
  10.5 0.0 collective-permute-start.3
  10.5 0.0 collective-permute-done.1.mb
  10.5 0.7 %shard_map.119 = (bf16[272,128]{1,0:T(8,128)(2,1)S(1)}, bf16[256,128]{1,0:T(8,128)(2,1)S(1)}, bf16[256,256]{1,0:T(8,128)(2,1)S(1)}, f32[8,256]{1,0:T(8,128)S(1)}, f32[24,128]{1,0:T(8,128)S(1)}) custom-call(f32[1,8]{1,0:T(1,128)S(1)} %get-tuple-element.46.bias, f32[1,8]{1,0:T(1,128)S(1)} %get-tuple-element.47.alog, ...), custom_call_target="tpu_custom_call" | custom-call | tf_op jit(solution)/shard_map/pallas_call | solution.py:533
  11.1 0.1 collective-permute-start.7
  11.2 3.2 %collective-permute-done.3.rest_0_ = bf16[128,128]{1,0:T(8,128)(2,1)S(1)} collective-permute-done((bf16[128,128]{1,0:T(8,128)(2,1)S(1)}, bf16[128,128]{1,0:T(8,128)(2,1)S(1)}, u32[]{:S(2)}, u32[]{:S(2)}) %collective-permute-start.3) | collective-permute-done | bytes 32800 | tf_op jit(solution)/shard_map/ppermute | solution.py:479
  14.4 0.0 collective-permute-done.4.rest_1_
  14.4 0.0 collective-permute-done.5.rest_2_
  14.4 0.0 collective-permute-done.6.rest_3_
  14.4 0.6 %shard_map.120 = (bf16[256,128]{1,0:T(8,128)(2,1)S(1)}, bf16[256,256]{1,0:T(8,128)(2,1)S(1)}, f32[8,256]{1,0:T(8,128)S(1)}, f32[24,128]{1,0:T(8,128)S(1)}, bf16[...) custom-call(bf16[256,128]{1,0:T(8,128)(2,1)S(1)} %get-tuple-element., ...), custom_call_target="tpu_custom_call", output_to_operand_aliasing={{0}: (0, {}), {1}: (1, {}), {2}: (2, {}), {3}: (3, {})} | custom-call | flops 1073741824 | bytes 4194304 | tf_op jit(solution)/shard_map/pallas_call | solution.py:558
  15.0 1.2 %collective-permute-start.11 = (bf16[64,128]{1,0:T(8,128)(2,1)S(1)}, bf16[64,128]{1,0:T(8,128)(2,1)S(1)}, u32[]{:S(2)}, u32[]{:S(2)}) collective-permute-start(bf16[64,128]{1,0:T(8,128)(2,1)S(1)} %get-tuple-element.77), channel_id=1, source_target_pairs={{0,6},{1,7},{2,4},{3,5},{4,2},{5,3},{6,0},{7,1},{8,9},{9,8},{10,11... | collective-permute-start | bytes 49160 | tf_op jit(solution)/shard_map/ppermute | solution.py:479
  16.2 0.3 %collective-permute-start.12 = (bf16[64,128]{1,0:T(8,128)(2,1)S(1)}, bf16[64,128]{1,0:T(8,128)(2,1)S(1)}, u32[]{:S(2)}, u32[]{:S(2)}) collective-permute-start(bf16[64,128]{1,0:T(8,128)(2,1)S(1)} %get-tuple-element.78), channel_id=1, source_target_pairs={{0,4},{1,5},{2,6},{3,7},{4,0},{5,1},{6,2},{7,3},{8,9},{9,8},{10,11... | collective-permute-start | bytes 49160 | tf_op jit(solution)/shard_map/ppermute | solution.py:479
  16.6 2.0 %collective-permute-start.13 = (bf16[64,128]{1,0:T(8,128)(2,1)S(1)}, bf16[64,128]{1,0:T(8,128)(2,1)S(1)}, u32[]{:S(2)}, u32[]{:S(2)}) collective-permute-start(bf16[64,128]{1,0:T(8,128)(2,1)S(1)} %get-tuple-element.79), channel_id=1, source_target_pairs={{0,2},{1,3},{2,0},{3,1},{4,6},{5,7},{6,4},{7,5},{8,9},{9,8},{10,11... | collective-permute-start | bytes 49160 | tf_op jit(solution)/shard_map/ppermute | solution.py:479
  18.6 0.0 collective-permute-done.7.arrived
  18.6 0.4 %shard_map.121 = (bf16[64,128]{1,0:T(8,128)(2,1)S(1)}, bf16[64,128]{1,0:T(8,128)(2,1)S(1)}, bf16[64,128]{1,0:T(8,128)(2,1)S(1)}, bf16[64,128]{1,0:T(8,128)(2,1)S(1)}) custom-call(bf16[4,128]{1,0:T(4,128)(2,1)S(1)} %get-tuple-element.43.taps_x, bf16[4,256]{1,0:T(4,128)(2,1)S(1)} %get-tuple-element.44.taps_b, bf16[4,256]{1,0:T(4,128)(2,1)S(1)} %get-tuple-element.45.taps_c, ...), custom_call_target="tpu_custom_call" | custom-call | tf_op jit(solution)/shard_map/pallas_call | solution.py:581
  19.0 0.1 collective-permute-start.8
  19.1 0.5 %collective-permute-start.9 = (bf16[64,128]{1,0:T(8,128)(2,1)S(1)}, bf16[64,128]{1,0:T(8,128)(2,1)S(1)}, u32[]{:S(2)}, u32[]{:S(2)}) collective-permute-start(bf16[64,128]{1,0:T(8,128)(2,1)S(1)} %get-tuple-element.74), channel_id=1, source_target_pairs={{0,1},{1,0},{2,3},{3,2},{4,5},{5,4},{6,7},{7,6},{8,12},{9,13},{10,... | collective-permute-start | bytes 49160 | tf_op jit(solution)/shard_map/ppermute | solution.py:479
  19.6 0.1 collective-permute-done.11.ea
  19.7 0.2 %collective-permute-done.12.eb = bf16[64,128]{1,0:T(8,128)(2,1)S(1)} collective-permute-done((bf16[64,128]{1,0:T(8,128)(2,1)S(1)}, bf16[64,128]{1,0:T(8,128)(2,1)S(1)}, u32[]{:S(2)}, u32[]{:S(2)}) %collective-permute-start.12) | collective-permute-done | bytes 16416 | tf_op jit(solution)/shard_map/ppermute | solution.py:479
  20.0 0.3 %collective-permute-done.13.ec = bf16[64,128]{1,0:T(8,128)(2,1)S(1)} collective-permute-done((bf16[64,128]{1,0:T(8,128)(2,1)S(1)}, bf16[64,128]{1,0:T(8,128)(2,1)S(1)}, u32[]{:S(2)}, u32[]{:S(2)}) %collective-permute-start.13) | collective-permute-done | bytes 16416 | tf_op jit(solution)/shard_map/ppermute | solution.py:479
  20.3 0.0 collective-permute-done.8.ra
  20.3 0.2 collective-permute-done.9.rb
  20.5 0.5 %collective-permute-done.10.rc = bf16[64,128]{1,0:T(8,128)(2,1)S(1)} collective-permute-done((bf16[64,128]{1,0:T(8,128)(2,1)S(1)}, bf16[64,128]{1,0:T(8,128)(2,1)S(1)}, u32[]{:S(2)}, u32[]{:S(2)}) %collective-permute-start.10) | collective-permute-done | bytes 16416 | tf_op jit(solution)/shard_map/ppermute | solution.py:479
  20.9 0.8 %shard_map.122 = bf16[64,512]{1,0:T(8,128)(2,1)} custom-call(bf16[64,128]{1,0:T(8,128)(2,1)S(1)} %get-tuple-element.72.o0, bf16[64,128]{1,0:T(8,128)(2,1)S(1)} %collective-permute-done.8.ra, bf16[64,128]{1,0:T(8,128)(2,1)S(1)} %collective-permute-done.9.rb, bf16[64,128]{1,0:T(8,128)(2,1)S(1)} %collective-permute-done.10.rc, ...), custom_call_target="tpu_custom_call" | custom-call | tf_op jit(solution)/shard_map/pallas_call | solution.py:597
  (4 shorter events, 0.0 us)
Async XLA Ops:
  1.3 6.0 %collective-permute-start.2 = (bf16[216,128]{1,0:T(8,128)(2,1)S(1)}, bf16[216,128]{1,0:T(8,128)(2,1)S(1)}, u32[]{:S(2)}, u32[]{:S(2)}) collective-permute-start(bf16[216,128]{1,0:T(8,128)(2,1)S(1)} %get-tuple-element.51), channel_id=1, source_target_pairs={{0,2},{1,3},{2,0},{3,1},{4,6},{5,7},{6,4},{7,5},{8,9},{9,8},{10,11... | collective-permute-start | bytes 165896 | tf_op jit(solution)/shard_map/ppermute | solution.py:479
  4.3 6.1 %collective-permute-start = (bf16[328,128]{1,0:T(8,128)(2,1)S(1)}, bf16[328,128]{1,0:T(8,128)(2,1)S(1)}, u32[]{:S(2)}, u32[]{:S(2)}) collective-permute-start(bf16[328,128]{1,0:T(8,128)(2,1)S(1)} %get-tuple-element.49), channel_id=1, source_target_pairs={{0,6},{1,7},{2,4},{3,5},{4,2},{5,3},{6,0},{7,1},{8,9},{9,8},{10,11... | collective-permute-start | bytes 251912 | tf_op jit(solution)/shard_map/ppermute | solution.py:479
  5.9 4.6 %collective-permute-start.1 = (bf16[328,128]{1,0:T(8,128)(2,1)S(1)}, bf16[328,128]{1,0:T(8,128)(2,1)S(1)}, u32[]{:S(2)}, u32[]{:S(2)}) collective-permute-start(bf16[328,128]{1,0:T(8,128)(2,1)S(1)} %get-tuple-element.50), channel_id=1, source_target_pairs={{0,4},{1,5},{2,6},{3,7},{4,0},{5,1},{6,2},{7,3},{8,9},{9,8},{10,11... | collective-permute-start | bytes 251912 | tf_op jit(solution)/shard_map/ppermute | solution.py:479
  5.9 8.5 %collective-permute-start.4 = (bf16[328,128]{1,0:T(8,128)(2,1)S(1)}, bf16[328,128]{1,0:T(8,128)(2,1)S(1)}, u32[]{:S(2)}, u32[]{:S(2)}) collective-permute-start(bf16[328,128]{1,0:T(8,128)(2,1)S(1)} %get-tuple-element.58), channel_id=1, source_target_pairs={{0,1},{1,0},{2,3},{3,2},{4,5},{5,4},{6,7},{7,6},{8,14},{9,15},{10,... | collective-permute-start | bytes 251912 | tf_op jit(solution)/shard_map/ppermute | solution.py:479
  5.9 8.5 %collective-permute-start.5 = (bf16[328,128]{1,0:T(8,128)(2,1)S(1)}, bf16[328,128]{1,0:T(8,128)(2,1)S(1)}, u32[]{:S(2)}, u32[]{:S(2)}) collective-permute-start(bf16[328,128]{1,0:T(8,128)(2,1)S(1)} %get-tuple-element.59), channel_id=1, source_target_pairs={{0,1},{1,0},{2,3},{3,2},{4,5},{5,4},{6,7},{7,6},{8,12},{9,13},{10,... | collective-permute-start | bytes 251912 | tf_op jit(solution)/shard_map/ppermute | solution.py:479
  7.3 7.1 %collective-permute-start.6 = (bf16[328,128]{1,0:T(8,128)(2,1)S(1)}, bf16[328,128]{1,0:T(8,128)(2,1)S(1)}, u32[]{:S(2)}, u32[]{:S(2)}) collective-permute-start(bf16[328,128]{1,0:T(8,128)(2,1)S(1)} %get-tuple-element.60), channel_id=1, source_target_pairs={{0,1},{1,0},{2,3},{3,2},{4,5},{5,4},{6,7},{7,6},{8,10},{9,11},{10,... | collective-permute-start | bytes 251912 | tf_op jit(solution)/shard_map/ppermute | solution.py:479
  10.5 3.9 %collective-permute-start.3 = (bf16[128,128]{1,0:T(8,128)(2,1)S(1)}, bf16[128,128]{1,0:T(8,128)(2,1)S(1)}, u32[]{:S(2)}, u32[]{:S(2)}) collective-permute-start(bf16[128,128]{1,0:T(8,128)(2,1)S(1)} %get-tuple-element.57), channel_id=1, source_target_pairs={{0,2},{1,3},{2,0},{3,1},{4,6},{5,7},{6,4},{7,5},{8,9},{9,8},{10,11... | collective-permute-start | bytes 98312 | tf_op jit(solution)/shard_map/ppermute | solution.py:479
  11.1 7.5 %collective-permute-start.7 = (bf16[272,128]{1,0:T(8,128)(2,1)S(1)}, bf16[272,128]{1,0:T(8,128)(2,1)S(1)}, u32[]{:S(2)}, u32[]{:S(2)}) collective-permute-start(bf16[272,128]{1,0:T(8,128)(2,1)S(1)} %get-tuple-element.71), channel_id=1, source_target_pairs={{0,8},{2,10},{4,12},{6,14},{8,0},{10,2},{12,4},{14,6},{1,9},{3,11}... | collective-permute-start | bytes 208904 | tf_op jit(solution)/shard_map/ppermute | solution.py:555
  15.0 4.7 %collective-permute-start.11 = (bf16[64,128]{1,0:T(8,128)(2,1)S(1)}, bf16[64,128]{1,0:T(8,128)(2,1)S(1)}, u32[]{:S(2)}, u32[]{:S(2)}) collective-permute-start(bf16[64,128]{1,0:T(8,128)(2,1)S(1)} %get-tuple-element.77), channel_id=1, source_target_pairs={{0,6},{1,7},{2,4},{3,5},{4,2},{5,3},{6,0},{7,1},{8,9},{9,8},{10,11... | collective-permute-start | bytes 49160 | tf_op jit(solution)/shard_map/ppermute | solution.py:479
  16.2 3.7 %collective-permute-start.12 = (bf16[64,128]{1,0:T(8,128)(2,1)S(1)}, bf16[64,128]{1,0:T(8,128)(2,1)S(1)}, u32[]{:S(2)}, u32[]{:S(2)}) collective-permute-start(bf16[64,128]{1,0:T(8,128)(2,1)S(1)} %get-tuple-element.78), channel_id=1, source_target_pairs={{0,4},{1,5},{2,6},{3,7},{4,0},{5,1},{6,2},{7,3},{8,9},{9,8},{10,11... | collective-permute-start | bytes 49160 | tf_op jit(solution)/shard_map/ppermute | solution.py:479
  16.6 3.7 %collective-permute-start.13 = (bf16[64,128]{1,0:T(8,128)(2,1)S(1)}, bf16[64,128]{1,0:T(8,128)(2,1)S(1)}, u32[]{:S(2)}, u32[]{:S(2)}) collective-permute-start(bf16[64,128]{1,0:T(8,128)(2,1)S(1)} %get-tuple-element.79), channel_id=1, source_target_pairs={{0,2},{1,3},{2,0},{3,1},{4,6},{5,7},{6,4},{7,5},{8,9},{9,8},{10,11... | collective-permute-start | bytes 49160 | tf_op jit(solution)/shard_map/ppermute | solution.py:479
  18.6 2.3 %copy-start = (bf16[64,512]{1,0:T(8,128)(2,1)S(1)}, bf16[64,512]{1,0:T(8,128)(2,1)}, u32[]{:S(2)}) copy-start(bf16[64,512]{1,0:T(8,128)(2,1)} %z.1) | copy-start | bytes 196612
  19.0 1.3 %collective-permute-start.8 = (bf16[64,128]{1,0:T(8,128)(2,1)S(1)}, bf16[64,128]{1,0:T(8,128)(2,1)S(1)}, u32[]{:S(2)}, u32[]{:S(2)}) collective-permute-start(bf16[64,128]{1,0:T(8,128)(2,1)S(1)} %get-tuple-element.73), channel_id=1, source_target_pairs={{0,1},{1,0},{2,3},{3,2},{4,5},{5,4},{6,7},{7,6},{8,14},{9,15},{10,... | collective-permute-start | bytes 49160 | tf_op jit(solution)/shard_map/ppermute | solution.py:479
  19.1 1.3 %collective-permute-start.9 = (bf16[64,128]{1,0:T(8,128)(2,1)S(1)}, bf16[64,128]{1,0:T(8,128)(2,1)S(1)}, u32[]{:S(2)}, u32[]{:S(2)}) collective-permute-start(bf16[64,128]{1,0:T(8,128)(2,1)S(1)} %get-tuple-element.74), channel_id=1, source_target_pairs={{0,1},{1,0},{2,3},{3,2},{4,5},{5,4},{6,7},{7,6},{8,12},{9,13},{10,... | collective-permute-start | bytes 49160 | tf_op jit(solution)/shard_map/ppermute | solution.py:479
  19.7 1.2 %collective-permute-start.10 = (bf16[64,128]{1,0:T(8,128)(2,1)S(1)}, bf16[64,128]{1,0:T(8,128)(2,1)S(1)}, u32[]{:S(2)}, u32[]{:S(2)}) collective-permute-start(bf16[64,128]{1,0:T(8,128)(2,1)S(1)} %get-tuple-element.75), channel_id=1, source_target_pairs={{0,1},{1,0},{2,3},{3,2},{4,5},{5,4},{6,7},{7,6},{8,10},{9,11},{10,... | collective-permute-start | bytes 49160 | tf_op jit(solution)/shard_map/ppermute | solution.py:479
